TPU v7x, 32 devices: a whole 2x2x4 slice. The times are simulated.
32 devices in a mesh: dom: 4 (over y, x), orb: 8 (over z, core).
Axes of the slice: x: 2, y: 2, z: 4, core: 2. Of those that a mesh axis runs over, the one named last changes fastest.
Arguments:
- orbitals: float32 [32, 32, 768], P('dom', 'orb'), may hold values from -24 to 24
- potential: float32 [32, 768], P('dom'), may hold values from -2 to 2
Outputs:
- gram_blocks: float32 [2, 32, 32], P(None, 'orb', 'dom')
All inputs are finite; a program needn't handle non-finite values.
Results may differ from a plain program's by a relative error of at most 0.00005.
Values sent between devices are 32-bit elements; how exact they have to be, the bound alone decides.
No kernel may reach another device: no remote copies, remote signals or barrier semaphores. Data moves between devices by JAX's collectives and lax.ppermute only.
A program may use at most 64 MiB of HBM per device.

v0:
```python
import functools

import jax
import jax.numpy as jnp
import numpy as np
from jax import lax
from jax.experimental import pallas as pl
from jax.experimental.pallas import tpu as pltpu
from jax.sharding import PartitionSpec as P


NZ = 96
NY = 8
RADIUS = 6
LANES = 128


coeffs = (
    -5369.0 / 1800.0,
    12.0 / 7.0,
    -15.0 / 56.0,
    10.0 / 189.0,
    -1.0 / 112.0,
    2.0 / 1925.0,
    -1.0 / 16632.0,
)
center_value = 6.5
half_value = 6.5


def turned(tile, shift, axis=1):
    shift = shift % tile.shape[axis]
    return tile if shift == 0 else pltpu.roll(tile, shift, axis)


def line_of(flat, row, lane):
    first, offset = divmod(row * NZ, LANES)
    line = turned(flat[:, first * LANES : (first + 1) * LANES], -offset)
    if offset + NZ > LANES:
        after = turned(flat[:, (first + 1) * LANES : (first + 2) * LANES], -offset)
        line = jnp.where(lane < LANES - offset, line, after)
    return jnp.where(lane < NZ, line, 0.0)


Z_FACTOR = 1.09375


def z_matrix():
    matrix = np.zeros((LANES, LANES), np.float64)
    for cell in range(NZ):
        for step in range(1, RADIUS + 1):
            matrix[cell, (cell + step) % NZ] += coeffs[step] * Z_FACTOR
            matrix[cell, (cell - step) % NZ] += coeffs[step] * Z_FACTOR
    leading = matrix.astype(jnp.bfloat16)
    trailing = (matrix - leading.astype(np.float64)).astype(jnp.bfloat16)
    both = np.concatenate([leading, trailing], axis=1)
    return np.concatenate([both, both], axis=0)


def stencil(load, at, along_z, scale):
    tile = load(at)
    rows = {s: turned(tile, s, 0) + turned(tile, -s, 0) for s in (1, 2, 3)}
    middle = turned(tile, 4, 0)
    rows[4] = middle + middle
    rows[5], rows[6] = rows[3], rows[2]
    total = (scale / Z_FACTOR) * along_z
    for step in range(1, RADIUS + 1):
        near = load(at + step) + load(at - step) + rows[step]
        total = total + (scale * coeffs[step]) * near
    return total


def pack_kernel(orbitals_ref, potential_ref, out_ref, held_ref, sems):
    planes, count, cells = orbitals_ref.shape
    field = pltpu.make_async_copy(orbitals_ref, out_ref.at[pl.ds(0, planes)], sems.at[0])
    level = pltpu.make_async_copy(potential_ref, held_ref, sems.at[1])
    level.start()
    field.start()
    level.wait()
    out_ref[pl.ds(planes, planes // count)] = held_ref[...].reshape(planes // count, count, cells)
    field.wait()


def filter_kernel(matrix_ref, *refs):
    blocks, refs = refs[:-8], refs[-8:]
    out_ref, grid_ref, one_ref, two_ref, three_ref, four_ref, z_ref, save_ref = refs
    count, planes = blocks[0].shape[1], out_ref.shape[0] // (2 * blocks[0].shape[1])
    total = planes * len(blocks)
    lane = lax.broadcasted_iota(jnp.int32, (NY, LANES), 1)

    dom = lax.axis_index("dom")
    for index, block in enumerate(blocks):
        place = pl.multiple_of((((dom ^ index) - dom) & (len(blocks) - 1)) * planes * NY, planes * NY)
        for q in range(count + 1):
            if q < count:
                flat = block[pl.ds(0, planes), q, :]
            else:
                flat = block[pl.ds(planes, planes // count)].reshape(planes, block.shape[2])
            for row in range(NY):
                line = line_of(flat, row, lane)
                if q == count:
                    line = (line - center_value - 1.5 * coeffs[0]) / half_value
                grid_ref[q, pl.ds(place + row, planes, stride=NY), :] = line

    def tile_of(ref):
        def load(at):
            return ref[pl.ds((at % total) * NY, NY), :]

        return load

    def level(at):
        return grid_ref[count, pl.ds((at % total) * NY, NY), :]

    def z_pass(ref, first, number):
        cells = pl.ds(first * NY, number * NY)
        value = ref[cells, :]
        upper = value.astype(jnp.bfloat16)
        lower = (value - upper.astype(jnp.float32)).astype(jnp.bfloat16)
        product = jnp.dot(
            jnp.concatenate([upper, lower], axis=1),
            matrix_ref[...],
            preferred_element_type=jnp.float32,
        )
        z_ref[cells, :] = product[:, :LANES] + product[:, LANES:]

    small = -0.5 / half_value

    def one_orbital(orb, carry):
        start = tile_of(grid_ref.at[orb])
        one, two, three, four = (tile_of(r) for r in (one_ref, two_ref, three_ref, four_ref))
        along_z = tile_of(z_ref)

        def put(ref, at, value):
            ref[pl.ds((at % total) * NY, NY), :] = value

        z_pass(grid_ref.at[orb], 0, total)
        for at in range(total):
            put(one_ref, at, stencil(start, at, along_z(at), small) + level(at) * start(at))
        z_pass(one_ref, 0, total)
        for at in range(total):
            twice = level(at) + level(at)
            value = stencil(one, at, along_z(at), 2.0 * small) + twice * one(at)
            put(two_ref, at, value - start(at))
        z_pass(two_ref, 0, total)
        for at in range(total):
            put(three_ref, at, stencil(two, at, along_z(at), small) + level(at) * two(at))
        z_pass(three_ref, 0, planes + RADIUS)
        z_pass(three_ref, total - RADIUS, RADIUS)
        for at in range(-RADIUS, planes + RADIUS):
            twice = level(at) + level(at)
            value = stencil(three, at, along_z(at), 2.0 * small) + twice * three(at)
            put(four_ref, at, value - two(at))
        z_pass(four_ref, 0, planes)
        for at in range(planes):
            scaled = stencil(four, at, along_z(at), small) + level(at) * four(at)
            save_ref[orb, pl.ds(at * NY, NY), :] = four(at)
            save_ref[count + orb, pl.ds(at * NY, NY), :] = (
                half_value * scaled + center_value * four(at)
            )
        return carry

    lax.fori_loop(0, count, one_orbital, 0)

    rows = 2 * count
    for at in range(planes):
        lines = [save_ref[:, at * NY + row, :] for row in range(NY)]
        for tile in range(NY * NZ // LANES):
            first = tile * LANES
            value = None
            for row in range(NY):
                low, high = max(row * NZ, first), min((row + 1) * NZ, first + LANES)
                if low >= high:
                    continue
                piece = turned(lines[row], row * NZ - first)
                value = piece if value is None else jnp.where(lane < low - first, value, piece)
            out_ref[pl.ds(at * rows, rows), first : first + LANES] = value


def split(value):
    upper = value.astype(jnp.bfloat16)
    lower = (value - upper.astype(jnp.float32)).astype(jnp.bfloat16)
    return upper, lower


def products(left, units, planes, count):
    upper, lower = split(left)
    cells = left.shape[1]
    lines = [
        jnp.zeros((planes * count, cells), jnp.float32)
        if unit is None
        else unit[pl.ds(0, planes)].reshape(planes * count, cells)
        for unit in units
    ]
    right_upper, right_lower = split(jnp.concatenate(lines, axis=0))

    def product(one, two):
        return lax.dot_general(
            one, two, (((1,), (1,)), ((), ())), preferred_element_type=jnp.float32
        )

    number = left.shape[0]
    full = product(jnp.concatenate([upper, lower], axis=0), right_upper)
    full = full[:number] + (full[number:] + product(upper, right_lower))
    rows = 2 * count
    plane_of = lax.broadcasted_iota(jnp.int32, (rows, full.shape[1]), 1)
    plane_of = (plane_of % (planes * count)) // count
    total = None
    for at in range(planes):
        part = jnp.where(plane_of == at, full[at * rows : (at + 1) * rows], 0.0)
        total = part if total is None else total + part
    return total


def early_kernel(left_ref, *refs, planes, count):
    units, out_ref = refs[:-1], refs[-1]
    half = len(units) // 2
    listed = (*units[:half], None, *units[half:], None)
    out_ref[...] = products(left_ref[...], listed, planes, count)


def late_kernel(left_ref, early_ref, near_ref, far_ref, out_ref, *, planes, count, flips, total_cells):
    line = planes * count
    late = products(left_ref[...], (near_ref, far_ref), planes, count) * (1.0 / total_cells)
    early = early_ref[...] * (1.0 / total_cells)
    width = early.shape[1] // 2
    rows = late.shape[0]
    lane = lax.broadcasted_iota(jnp.int32, (rows, width), 1)
    late = jnp.concatenate([late, jnp.zeros((rows, width - 2 * line), jnp.float32)], axis=1)
    halves = []
    for index in range(2):
        moved = turned(late, width - (1 + index) * line)
        part = early[:, index * width : (index + 1) * width]
        part = jnp.where(lane < width - line, part, moved)
        step = count
        while step < line:
            part = part + turned(part, -step)
            step *= 2
        halves.append(part)
    dom, orb = lax.axis_index("dom"), lax.axis_index("orb")
    chip, core = orb >> 1, orb & 1
    even = jnp.where(core == 0, halves[0], halves[1])
    odd = jnp.where(core == 0, halves[1], halves[0])
    joined = jnp.where(lane % line < count, even, turned(odd, count))
    for slot, flip in enumerate(flips):
        out_ref[chip ^ flip ^ dom] = turned(joined, -slot * line)


def sum_kernel(*refs):
    parts, out_ref = refs[:-1], refs[-1]
    total = parts[0][...]
    for part in parts[1:]:
        total = total + part[...]
    first, rows, columns = out_ref.shape
    for index in range(first):
        out_ref[index] = total[index * rows : (index + 1) * rows, :columns]


VMEM = pl.BlockSpec(memory_space=pltpu.VMEM)
HBM = pl.BlockSpec(memory_space=pltpu.HBM)
SMALL = pltpu.CompilerParams(vmem_limit_bytes=8 << 20)


def gathered_device(orbitals, potential):
    return gathered_steps(orbitals, potential)


def gathered_steps(orbitals, potential):
    doms, orbs = lax.axis_size("dom"), lax.axis_size("orb")
    chips = orbs // 2
    planes, count, cells = orbitals.shape
    total = planes * doms

    def swap_orb(value, flip):
        return lax.ppermute(value, "orb", [(i, i ^ flip) for i in range(orbs)])

    def along_dom(value, step):
        return lax.ppermute(value, "dom", [(i, i ^ step) for i in range(doms)])

    packed = pl.pallas_call(
        pack_kernel,
        out_shape=jax.ShapeDtypeStruct((planes + planes // count, count, cells), jnp.float32),
        in_specs=[HBM, HBM],
        out_specs=VMEM,
        scratch_shapes=[pltpu.VMEM((planes, cells), jnp.float32), pltpu.SemaphoreType.DMA((2,))],
        compiler_params=SMALL,
        name="pack",
    )(
        pltpu.with_memory_space_constraint(orbitals, pltpu.HBM),
        pltpu.with_memory_space_constraint(potential, pltpu.HBM),
    )
    others = {step: along_dom(packed, step) for step in range(1, doms)}
    blocks = [packed] + [others[step] for step in range(1, doms)]

    flips = (0, *FLIPS) if chips == 1 + len(FLIPS) else tuple(range(chips))
    near = {0: packed}
    for flip in flips[1:]:
        near[flip] = swap_orb(orbitals, 2 * flip)
    far = {0: swap_orb(orbitals, 1)}
    for flip in flips[1:]:
        if flip == CROSS:
            far[flip] = swap_orb(orbitals, 2 * flip + 1)
        else:
            far[flip] = swap_orb(near[flip], 1)

    apps = count * (3 * total + 2 * planes + 2 * RADIUS)
    left = pl.pallas_call(
        filter_kernel,
        out_shape=jax.ShapeDtypeStruct((planes * 2 * count, cells), jnp.float32),
        in_specs=[VMEM] * (1 + doms),
        out_specs=VMEM,
        scratch_shapes=[pltpu.VMEM((count + 1, total * NY, LANES), jnp.float32)]
        + [pltpu.VMEM((total * NY, LANES), jnp.float32)] * 5
        + [pltpu.VMEM((2 * count, planes * NY, LANES), jnp.float32)],
        compiler_params=SMALL,
        cost_estimate=pl.CostEstimate(
            flops=apps * NY * LANES * 50,
            bytes_accessed=(count + 1) * total * cells * 4,
            transcendentals=0,
        ),
        name="filter",
    )(jnp.asarray(z_matrix()), *blocks)

    first = flips[:-1]
    early = pl.pallas_call(
        functools.partial(early_kernel, planes=planes, count=count),
        out_shape=jax.ShapeDtypeStruct((2 * count, 2 * chips * planes * count), jnp.float32),
        in_specs=[VMEM] * (1 + 2 * len(first)),
        out_specs=VMEM,
        compiler_params=SMALL,
        name="early",
    )(left, *[near[flip] for flip in first], *[far[flip] for flip in first])

    shares = pl.pallas_call(
        functools.partial(
            late_kernel, planes=planes, count=count, flips=flips, total_cells=total * cells
        ),
        out_shape=jax.ShapeDtypeStruct((doms, 2 * count, LANES), jnp.float32),
        in_specs=[VMEM] * 4,
        out_specs=VMEM,
        compiler_params=SMALL,
        name="late",
    )(left, early, near[flips[-1]], far[flips[-1]])
    parts = [shares[0]] + [along_dom(shares[k], k) for k in range(1, doms)]
    return pl.pallas_call(
        sum_kernel,
        out_shape=jax.ShapeDtypeStruct((2, count, orbs * count // doms), jnp.float32),
        in_specs=[VMEM] * doms,
        out_specs=VMEM,
        compiler_params=SMALL,
        name="total",
    )(*parts)


def with_halo(cells, sides, width):
    for axis, dim in sides:
        count = lax.axis_size(axis)
        head = lax.slice_in_dim(cells, 0, width, axis=dim)
        tail = lax.slice_in_dim(cells, cells.shape[dim] - width, cells.shape[dim], axis=dim)
        cells = jnp.concatenate(
            [
                lax.ppermute(tail, axis, [(i, (i + 1) % count) for i in range(count)]),
                cells,
                lax.ppermute(head, axis, [((i + 1) % count, i) for i in range(count)]),
            ],
            axis=dim,
        )
    return cells


def periodic_pad(cube, axis_index):
    extent = cube.shape[axis_index]
    lower = lax.slice_in_dim(cube, extent - RADIUS, extent, axis=axis_index)
    upper = lax.slice_in_dim(cube, 0, RADIUS, axis=axis_index)
    return jnp.concatenate([lower, cube, upper], axis=axis_index)


def stencil_apply(padded, potential, count):
    offset = (potential.shape[0] - count) // 2
    middle = padded[RADIUS : RADIUS + count]
    width = middle.shape[1]
    cube = middle.reshape(count, width, NY, NZ)
    y_padded = periodic_pad(cube, 2)
    z_padded = periodic_pad(cube, 3)
    lap = 3.0 * coeffs[0] * cube
    for step in range(1, 7):
        near = (
            padded[RADIUS + step : RADIUS + step + count]
            + padded[RADIUS - step : RADIUS - step + count]
        )
        near = near.reshape(count, width, NY, NZ)
        near = (
            near
            + y_padded[:, :, RADIUS - step : RADIUS - step + NY]
            + y_padded[:, :, RADIUS + step : RADIUS + step + NY]
        )
        near = (
            near
            + z_padded[:, :, :, RADIUS - step : RADIUS - step + NZ]
            + z_padded[:, :, :, RADIUS + step : RADIUS + step + NZ]
        )
        lap = lap + coeffs[step] * near
    return (-0.5 * lap).reshape(count, width, NY * NZ) + potential[
        offset : offset + count, None, :
    ] * middle


def apply_field(field, potential):
    padded = with_halo(field, (("dom", 0),), RADIUS)
    return stencil_apply(padded, potential, field.shape[0])


def on_device(orbitals, potential):
    planes = orbitals.shape[0]
    current = (apply_field(orbitals, potential) - center_value * orbitals) / half_value
    following = (
        2.0 * (apply_field(current, potential) - center_value * current) / half_value - orbitals
    )
    applied = apply_field(following, potential)
    filt_cells, appl_cells = (
        lax.all_to_all(following, "orb", split_axis=2, concat_axis=1, tiled=True),
        lax.all_to_all(applied, "orb", split_axis=2, concat_axis=1, tiled=True),
    )
    total_cells = planes * lax.axis_size("dom") * orbitals.shape[2]
    correlation = jnp.einsum(
        "xop,xqp->oq",
        filt_cells,
        filt_cells,
        precision=lax.Precision.HIGHEST,
        preferred_element_type=jnp.float32,
    )
    projected = jnp.einsum(
        "xop,xqp->oq",
        filt_cells,
        appl_cells,
        precision=lax.Precision.HIGHEST,
        preferred_element_type=jnp.float32,
    )
    partial_blocks = jnp.stack([correlation, projected]) / total_cells
    row_blocks = lax.psum_scatter(partial_blocks, "orb", scatter_dimension=1, tiled=True)
    return lax.psum_scatter(row_blocks, "dom", scatter_dimension=2, tiled=True)


def fits_gather(mesh):
    doms, orbs = mesh.shape["dom"], mesh.shape["orb"]
    return orbs == 2 * doms and doms == 4


FLIPS = (1, 2, 3)
CROSS = 1


def solution(mesh):
    gather = fits_gather(mesh)
    return jax.shard_map(
        gathered_device if gather else on_device,
        mesh=mesh,
        in_specs=(P("dom", "orb", None), P("dom", None)),
        out_specs=P(None, "orb", "dom"),
        check_vma=False,
    )
```

profile of v0, /device:TPU:0, one launch (start us, length us, event | category | flops | bytes accessed | tf_op | source)
XLA Modules:
  0.0 31.3 jit_solution(8852916181693136225)
XLA Ops:
  0.0 1.0 %pack.1.refs_0_ = f32[10,4,768]{2,1,0:T(4,128)S(1)} custom-call(f32[8,4,768]{2,1,0:T(4,128)} %orbitals_ref.1, f32[8,768]{1,0:T(8,128)} %potential_ref.1), custom_call_target="tpu_custom_call" | custom-call | tf_op jit(solution)/shard_map/pack/pallas_call | solution.py:279
  1.0 3.0 %collective-permute-start = (f32[10,4,768]{2,1,0:T(4,128)S(1)}, f32[10,4,768]{2,1,0:T(4,128)S(1)}, u32[]{:S(2)}, u32[]{:S(2)}) collective-permute-start(f32[10,4,768]{2,1,0:T(4,128)S(1)} %pack.1.refs_0_), channel_id=1, source_target_pairs={{0,8},{8,0},{16,24},{24,16},{1,9},{9,1},{17,25},{25,17},{2,10},{10... | collective-permute-start | bytes 368648 | tf_op jit(solution)/shard_map/ppermute | solution.py:277
  4.0 1.5 %collective-permute-start.1 = (f32[10,4,768]{2,1,0:T(4,128)S(1)}, f32[10,4,768]{2,1,0:T(4,128)S(1)}, u32[]{:S(2)}, u32[]{:S(2)}) collective-permute-start(f32[10,4,768]{2,1,0:T(4,128)S(1)} %pack.1.refs_0_), channel_id=1, source_target_pairs={{0,16},{8,24},{16,0},{24,8},{1,17},{9,25},{17,1},{25,9},{2,18},{10... | collective-permute-start | bytes 368648 | tf_op jit(solution)/shard_map/ppermute | solution.py:277
  5.5 0.0 collective-permute-start.2
  5.6 3.0 %collective-permute-start.4 = (f32[8,4,768]{2,1,0:T(4,128)S(1)}, f32[8,4,768]{2,1,0:T(4,128)S(1)}, u32[]{:S(2)}, u32[]{:S(2)}) collective-permute-start(f32[8,4,768]{2,1,0:T(4,128)S(1)} %copy-done.1), channel_id=1, source_target_pairs={{0,4},{1,5},{2,6},{3,7},{4,0},{5,1},{6,2},{7,3},{8,12},{9,13},{10,... | collective-permute-start | bytes 294920 | tf_op jit(solution)/shard_map/ppermute | solution.py:274
  8.6 1.3 %collective-permute-start.8 = (f32[8,4,768]{2,1,0:T(4,128)S(1)}, f32[8,4,768]{2,1,0:T(4,128)S(1)}, u32[]{:S(2)}, u32[]{:S(2)}) collective-permute-start(f32[8,4,768]{2,1,0:T(4,128)S(1)} %copy-done.1), channel_id=1, source_target_pairs={{0,6},{1,7},{2,4},{3,5},{4,2},{5,3},{6,0},{7,1},{8,14},{9,15},{10,... | collective-permute-start | bytes 294920 | tf_op jit(solution)/shard_map/ppermute | solution.py:274
  10.0 5.5 %collective-permute-done.4.refs_2_ = f32[8,4,768]{2,1,0:T(4,128)S(1)} collective-permute-done((f32[8,4,768]{2,1,0:T(4,128)S(1)}, f32[8,4,768]{2,1,0:T(4,128)S(1)}, u32[]{:S(2)}, u32[]{:S(2)}) %collective-permute-start.4) | collective-permute-done | bytes 98336 | tf_op jit(solution)/shard_map/ppermute | solution.py:274
  15.5 0.1 collective-permute-start.3
  15.6 0.0 collective-permute-done.8.near_ref
  15.6 0.0 collective-permute-start.5
  15.6 0.0 collective-permute-done.refs_1_
  15.6 2.1 %collective-permute-start.6 = (f32[8,4,768]{2,1,0:T(4,128)S(1)}, f32[8,4,768]{2,1,0:T(4,128)S(1)}, u32[]{:S(2)}, u32[]{:S(2)}) collective-permute-start(f32[8,4,768]{2,1,0:T(4,128)S(1)} %copy-done.1), channel_id=1, source_target_pairs={{0,3},{1,2},{2,1},{3,0},{4,7},{5,6},{6,5},{7,4},{8,11},{9,10},{10,... | collective-permute-start | bytes 294920 | tf_op jit(solution)/shard_map/ppermute | solution.py:274
  17.7 0.0 collective-permute-start.7
  17.8 0.5 %collective-permute-start.9 = (f32[8,4,768]{2,1,0:T(4,128)S(1)}, f32[8,4,768]{2,1,0:T(4,128)S(1)}, u32[]{:S(2)}, u32[]{:S(2)}) collective-permute-start(f32[8,4,768]{2,1,0:T(4,128)S(1)} %collective-permute-done.8.near_ref), channel_id=1, source_target_pairs={{0,1},{1,0},{2,3},{3,2},{4,5},{5,4},{6,7},{7,6},{8,9},{9,8},{10,11... | collective-permute-start | bytes 294920 | tf_op jit(solution)/shard_map/ppermute | solution.py:274
  18.3 3.8 %filter.1.left_ref = f32[64,768]{1,0:T(8,128)S(1)} custom-call(bf16[256,256]{1,0:T(8,128)(2,1)S(1)} %copy-done, f32[10,4,768]{2,1,0:T(4,128)S(1)} %pack.1.refs_0_, f32[10,4,768]{2,1,0:T(4,128)S(1)} %collective-permute-done.refs_1_, f32[10,4,768]{2,1,0:T(4,128)S(1)} %collective-permute-done.1.refs_2_, f32[10,4,768]{2,1,0:T(4,128)S(1)} %collective-permute-done.2.refs_3_), custom_call_target="tpu_custom_call" | custom-call | flops 25395200 | bytes 491520 | tf_op jit(solution)/shard_map/filter/pallas_call | solution.py:306
  22.1 0.4 %early.1.early_ref = f32[8,256]{1,0:T(8,128)S(1)} custom-call(f32[64,768]{1,0:T(8,128)S(1)} %filter.1.left_ref, f32[10,4,768]{2,1,0:T(4,128)S(1)} %pack.1.refs_0_, f32[8,4,768]{2,1,0:T(4,128)S(1)} %collective-permute-done.3.refs_1_, f32[8,4,768]{2,1,0:T(4,128)S(1)} %collective-permute-done.4.refs_2_, f32[8,4,768]{2,1,0:T(4,128)S(1)} %collective-permute-done.5.refs_3_, ...), custom_call_target="tpu_custom_call" | custom-call | tf_op jit(solution)/shard_map/early/pallas_call | solution.py:324
  22.5 0.6 %late.1 = f32[4,8,128]{2,1,0:T(8,128)S(1)} custom-call(f32[64,768]{1,0:T(8,128)S(1)} %filter.1.left_ref, f32[8,256]{1,0:T(8,128)S(1)} %early.1.early_ref, f32[8,4,768]{2,1,0:T(4,128)S(1)} %collective-permute-done.8.near_ref, f32[8,4,768]{2,1,0:T(4,128)S(1)} %collective-permute-done.9.far_ref), custom_call_target="tpu_custom_call" | custom-call | tf_op jit(solution)/shard_map/late/pallas_call | solution.py:333
  23.1 1.5 %collective-permute-start.10 = (f32[8,128]{1,0:T(8,128)S(1)}, f32[8,128]{1,0:T(8,128)S(1)}, u32[]{:S(2)}, u32[]{:S(2)}) collective-permute-start(f32[8,128]{1,0:T(8,128)S(1)} %get-tuple-element.7), channel_id=1, source_target_pairs={{0,8},{8,0},{16,24},{24,16},{1,9},{9,1},{17,25},{25,17},{2,10},{10... | collective-permute-start | bytes 12296 | tf_op jit(solution)/shard_map/ppermute | solution.py:277
  24.6 1.5 %collective-permute-start.11 = (f32[8,128]{1,0:T(8,128)S(1)}, f32[8,128]{1,0:T(8,128)S(1)}, u32[]{:S(2)}, u32[]{:S(2)}) collective-permute-start(f32[8,128]{1,0:T(8,128)S(1)} %get-tuple-element.6), channel_id=1, source_target_pairs={{0,16},{8,24},{16,0},{24,8},{1,17},{9,25},{17,1},{25,9},{2,18},{10... | collective-permute-start | bytes 12296 | tf_op jit(solution)/shard_map/ppermute | solution.py:277
  26.1 0.5 %collective-permute-start.12 = (f32[8,128]{1,0:T(8,128)S(1)}, f32[8,128]{1,0:T(8,128)S(1)}, u32[]{:S(2)}, u32[]{:S(2)}) collective-permute-start(f32[8,128]{1,0:T(8,128)S(1)} %get-tuple-element.5), channel_id=1, source_target_pairs={{0,24},{8,16},{16,8},{24,0},{1,25},{9,17},{17,9},{25,1},{2,26},{10... | collective-permute-start | bytes 12296 | tf_op jit(solution)/shard_map/ppermute | solution.py:277
  26.6 0.1 collective-permute-done.10.refs_1_
  26.7 1.5 %collective-permute-done.11.refs_2_ = f32[8,128]{1,0:T(8,128)S(1)} collective-permute-done((f32[8,128]{1,0:T(8,128)S(1)}, f32[8,128]{1,0:T(8,128)S(1)}, u32[]{:S(2)}, u32[]{:S(2)}) %collective-permute-start.11) | collective-permute-done | bytes 4128 | tf_op jit(solution)/shard_map/ppermute | solution.py:277
  28.2 2.4 %collective-permute-done.12.refs_3_ = f32[8,128]{1,0:T(8,128)S(1)} collective-permute-done((f32[8,128]{1,0:T(8,128)S(1)}, f32[8,128]{1,0:T(8,128)S(1)}, u32[]{:S(2)}, u32[]{:S(2)}) %collective-permute-start.12) | collective-permute-done | bytes 4128 | tf_op jit(solution)/shard_map/ppermute | solution.py:277
  30.7 0.6 %total.1 = f32[2,4,8]{2,1,0:T(4,128)} custom-call(f32[8,128]{1,0:T(8,128)S(1)} %get-tuple-element.8.refs_0_, f32[8,128]{1,0:T(8,128)S(1)} %collective-permute-done.10.refs_1_, f32[8,128]{1,0:T(8,128)S(1)} %collective-permute-done.11.refs_2_, f32[8,128]{1,0:T(8,128)S(1)} %collective-permute-done.12.refs_3_), custom_call_target="tpu_custom_call" | custom-call | tf_op jit(solution)/shard_map/total/pallas_call | solution.py:344
  (12 shorter events, 0.0 us)
Async XLA Ops:
  0.0 18.3 %copy-start = (bf16[256,256]{1,0:T(8,128)(2,1)S(1)}, bf16[256,256]{1,0:T(8,128)(2,1)}, u32[]{:S(2)}) copy-start(bf16[256,256]{1,0:T(8,128)(2,1)} %constant.2.clone.matrix_ref) | copy-start | bytes 393220
  0.0 5.6 %copy-start.1 = (f32[8,4,768]{2,1,0:T(4,128)S(1)}, f32[8,4,768]{2,1,0:T(4,128)}, u32[]{:S(2)}) copy-start(f32[8,4,768]{2,1,0:T(4,128)} %orbitals_ref.1) | copy-start | bytes 294916
  1.0 14.6 %collective-permute-start = (f32[10,4,768]{2,1,0:T(4,128)S(1)}, f32[10,4,768]{2,1,0:T(4,128)S(1)}, u32[]{:S(2)}, u32[]{:S(2)}) collective-permute-start(f32[10,4,768]{2,1,0:T(4,128)S(1)} %pack.1.refs_0_), channel_id=1, source_target_pairs={{0,8},{8,0},{16,24},{24,16},{1,9},{9,1},{17,25},{25,17},{2,10},{10... | collective-permute-start | bytes 368648 | tf_op jit(solution)/shard_map/ppermute | solution.py:277
  4.0 13.7 %collective-permute-start.1 = (f32[10,4,768]{2,1,0:T(4,128)S(1)}, f32[10,4,768]{2,1,0:T(4,128)S(1)}, u32[]{:S(2)}, u32[]{:S(2)}) collective-permute-start(f32[10,4,768]{2,1,0:T(4,128)S(1)} %pack.1.refs_0_), channel_id=1, source_target_pairs={{0,16},{8,24},{16,0},{24,8},{1,17},{9,25},{17,1},{25,9},{2,18},{10... | collective-permute-start | bytes 368648 | tf_op jit(solution)/shard_map/ppermute | solution.py:277
  5.5 12.2 %collective-permute-start.2 = (f32[10,4,768]{2,1,0:T(4,128)S(1)}, f32[10,4,768]{2,1,0:T(4,128)S(1)}, u32[]{:S(2)}, u32[]{:S(2)}) collective-permute-start(f32[10,4,768]{2,1,0:T(4,128)S(1)} %pack.1.refs_0_), channel_id=1, source_target_pairs={{0,24},{8,16},{16,8},{24,0},{1,25},{9,17},{17,9},{25,1},{2,26},{10... | collective-permute-start | bytes 368648 | tf_op jit(solution)/shard_map/ppermute | solution.py:277
  5.6 9.9 %collective-permute-start.4 = (f32[8,4,768]{2,1,0:T(4,128)S(1)}, f32[8,4,768]{2,1,0:T(4,128)S(1)}, u32[]{:S(2)}, u32[]{:S(2)}) collective-permute-start(f32[8,4,768]{2,1,0:T(4,128)S(1)} %copy-done.1), channel_id=1, source_target_pairs={{0,4},{1,5},{2,6},{3,7},{4,0},{5,1},{6,2},{7,3},{8,12},{9,13},{10,... | collective-permute-start | bytes 294920 | tf_op jit(solution)/shard_map/ppermute | solution.py:274
  8.6 7.0 %collective-permute-start.8 = (f32[8,4,768]{2,1,0:T(4,128)S(1)}, f32[8,4,768]{2,1,0:T(4,128)S(1)}, u32[]{:S(2)}, u32[]{:S(2)}) collective-permute-start(f32[8,4,768]{2,1,0:T(4,128)S(1)} %copy-done.1), channel_id=1, source_target_pairs={{0,6},{1,7},{2,4},{3,5},{4,2},{5,3},{6,0},{7,1},{8,14},{9,15},{10,... | collective-permute-start | bytes 294920 | tf_op jit(solution)/shard_map/ppermute | solution.py:274
  15.5 6.6 %collective-permute-start.3 = (f32[8,4,768]{2,1,0:T(4,128)S(1)}, f32[8,4,768]{2,1,0:T(4,128)S(1)}, u32[]{:S(2)}, u32[]{:S(2)}) collective-permute-start(f32[8,4,768]{2,1,0:T(4,128)S(1)} %copy-done.1), channel_id=1, source_target_pairs={{0,2},{1,3},{2,0},{3,1},{4,6},{5,7},{6,4},{7,5},{8,10},{9,11},{10,... | collective-permute-start | bytes 294920 | tf_op jit(solution)/shard_map/ppermute | solution.py:274
  15.6 6.5 %collective-permute-start.5 = (f32[8,4,768]{2,1,0:T(4,128)S(1)}, f32[8,4,768]{2,1,0:T(4,128)S(1)}, u32[]{:S(2)}, u32[]{:S(2)}) collective-permute-start(f32[8,4,768]{2,1,0:T(4,128)S(1)} %copy-done.1), channel_id=1, source_target_pairs={{0,1},{1,0},{2,3},{3,2},{4,5},{5,4},{6,7},{7,6},{8,9},{9,8},{10,11... | collective-permute-start | bytes 294920 | tf_op jit(solution)/shard_map/ppermute | solution.py:274
  15.6 6.5 %collective-permute-start.6 = (f32[8,4,768]{2,1,0:T(4,128)S(1)}, f32[8,4,768]{2,1,0:T(4,128)S(1)}, u32[]{:S(2)}, u32[]{:S(2)}) collective-permute-start(f32[8,4,768]{2,1,0:T(4,128)S(1)} %copy-done.1), channel_id=1, source_target_pairs={{0,3},{1,2},{2,1},{3,0},{4,7},{5,6},{6,5},{7,4},{8,11},{9,10},{10,... | collective-permute-start | bytes 294920 | tf_op jit(solution)/shard_map/ppermute | solution.py:274
  17.7 4.4 %collective-permute-start.7 = (f32[8,4,768]{2,1,0:T(4,128)S(1)}, f32[8,4,768]{2,1,0:T(4,128)S(1)}, u32[]{:S(2)}, u32[]{:S(2)}) collective-permute-start(f32[8,4,768]{2,1,0:T(4,128)S(1)} %collective-permute-done.4.refs_2_), channel_id=1, source_target_pairs={{0,1},{1,0},{2,3},{3,2},{4,5},{5,4},{6,7},{7,6},{8,9},{9,8},{10,11... | collective-permute-start | bytes 294920 | tf_op jit(solution)/shard_map/ppermute | solution.py:274
  17.8 4.7 %collective-permute-start.9 = (f32[8,4,768]{2,1,0:T(4,128)S(1)}, f32[8,4,768]{2,1,0:T(4,128)S(1)}, u32[]{:S(2)}, u32[]{:S(2)}) collective-permute-start(f32[8,4,768]{2,1,0:T(4,128)S(1)} %collective-permute-done.8.near_ref), channel_id=1, source_target_pairs={{0,1},{1,0},{2,3},{3,2},{4,5},{5,4},{6,7},{7,6},{8,9},{9,8},{10,11... | collective-permute-start | bytes 294920 | tf_op jit(solution)/shard_map/ppermute | solution.py:274
  23.1 3.6 %collective-permute-start.10 = (f32[8,128]{1,0:T(8,128)S(1)}, f32[8,128]{1,0:T(8,128)S(1)}, u32[]{:S(2)}, u32[]{:S(2)}) collective-permute-start(f32[8,128]{1,0:T(8,128)S(1)} %get-tuple-element.7), channel_id=1, source_target_pairs={{0,8},{8,0},{16,24},{24,16},{1,9},{9,1},{17,25},{25,17},{2,10},{10... | collective-permute-start | bytes 12296 | tf_op jit(solution)/shard_map/ppermute | solution.py:277
  24.6 3.6 %collective-permute-start.11 = (f32[8,128]{1,0:T(8,128)S(1)}, f32[8,128]{1,0:T(8,128)S(1)}, u32[]{:S(2)}, u32[]{:S(2)}) collective-permute-start(f32[8,128]{1,0:T(8,128)S(1)} %get-tuple-element.6), channel_id=1, source_target_pairs={{0,16},{8,24},{16,0},{24,8},{1,17},{9,25},{17,1},{25,9},{2,18},{10... | collective-permute-start | bytes 12296 | tf_op jit(solution)/shard_map/ppermute | solution.py:277
  26.1 4.5 %collective-permute-start.12 = (f32[8,128]{1,0:T(8,128)S(1)}, f32[8,128]{1,0:T(8,128)S(1)}, u32[]{:S(2)}, u32[]{:S(2)}) collective-permute-start(f32[8,128]{1,0:T(8,128)S(1)} %get-tuple-element.5), channel_id=1, source_target_pairs={{0,24},{8,16},{16,8},{24,0},{1,25},{9,17},{17,9},{25,1},{2,26},{10... | collective-permute-start | bytes 12296 | tf_op jit(solution)/shard_map/ppermute | solution.py:277
where the time goes:
time: 31.4 us; the launch traced here: 31.3 us
  starting transfers between devices  15.2 us (48%)
  waiting for transfers between devices  9.57 us (30%)
  Pallas kernels  6.39 us (20%)
    ppermute x6, starting transfers between devices, along_dom(): return lax.ppermute(value, 'dom', [(i, i ^ step) for i in range(doms)])  8.07 us
    ppermute x7, starting transfers between devices, swap_orb(): return lax.ppermute(value, 'orb', [(i, i ^ flip) for i in range(orbs)])  7.14 us
    ppermute x7, waiting for transfers between devices, swap_orb(): return lax.ppermute(value, 'orb', [(i, i ^ flip) for i in range(orbs)])  5.53 us
    ppermute x6, waiting for transfers between devices, along_dom(): return lax.ppermute(value, 'dom', [(i, i ^ step) for i in range(doms)])  4.04 us
    pallas_call x1, Pallas kernels, gathered_steps(): pl.pallas_call(filter_kernel, out_shape=jax.ShapeDtypeStruct((planes * 2...  3.79 us
    pallas_call x1, Pallas kernels, gathered_steps(): pl.pallas_call(pack_kernel, out_shape=jax.ShapeDtypeStruct((planes + plan...  0.98 us
    pallas_call x1, Pallas kernels, gathered_steps(): pl.pallas_call(functools.partial(late_kernel, planes=planes, count=count,...  0.64 us
  transfers between devices with their start and end apart: 13, of which 4 were waited for; matrix products, arithmetic and copies ran while one was open for 0% of the time, Pallas kernels for 13%

commit v1 on v0

--- a/solution.py
+++ b/solution.py
@@ -182,67 +182,49 @@
     return upper, lower
 
 
-def products(left, units, planes, count):
-    upper, lower = split(left)
-    cells = left.shape[1]
-    lines = [
-        jnp.zeros((planes * count, cells), jnp.float32)
-        if unit is None
-        else unit[pl.ds(0, planes)].reshape(planes * count, cells)
-        for unit in units
-    ]
-    right_upper, right_lower = split(jnp.concatenate(lines, axis=0))
-
-    def product(one, two):
-        return lax.dot_general(
-            one, two, (((1,), (1,)), ((), ())), preferred_element_type=jnp.float32
-        )
-
-    number = left.shape[0]
-    full = product(jnp.concatenate([upper, lower], axis=0), right_upper)
-    full = full[:number] + (full[number:] + product(upper, right_lower))
-    rows = 2 * count
-    plane_of = lax.broadcasted_iota(jnp.int32, (rows, full.shape[1]), 1)
-    plane_of = (plane_of % (planes * count)) // count
-    total = None
+def products(left_ref, units, planes):
+    rows = left_ref.shape[0] // planes
+    left, right = [], []
     for at in range(planes):
-        part = jnp.where(plane_of == at, full[at * rows : (at + 1) * rows], 0.0)
-        total = part if total is None else total + part
-    return total
-
-
-def early_kernel(left_ref, *refs, planes, count):
+        left.append(jnp.concatenate(split(left_ref[pl.ds(at * rows, rows), :]), axis=0))
+        lines = jnp.concatenate([unit[at] for unit in units], axis=0)
+        right.append(jnp.concatenate(split(lines), axis=0))
+    full = lax.dot_general(
+        jnp.concatenate(left, axis=1),
+        jnp.concatenate(right, axis=1),
+        (((1,), (1,)), ((), ())),
+        preferred_element_type=jnp.float32,
+    )
+    full = full[:rows] + full[rows:]
+    number = full.shape[1] // 2
+    return full[:, :number] + full[:, number:]
+
+
+def widened(value):
+    spare = jnp.zeros((value.shape[0], LANES - value.shape[1]), jnp.float32)
+    return jnp.concatenate([value, spare], axis=1)
+
+
+def near_kernel(left_ref, *refs, planes):
     units, out_ref = refs[:-1], refs[-1]
-    half = len(units) // 2
-    listed = (*units[:half], None, *units[half:], None)
-    out_ref[...] = products(left_ref[...], listed, planes, count)
-
-
-def late_kernel(left_ref, early_ref, near_ref, far_ref, out_ref, *, planes, count, flips, total_cells):
-    line = planes * count
-    late = products(left_ref[...], (near_ref, far_ref), planes, count) * (1.0 / total_cells)
-    early = early_ref[...] * (1.0 / total_cells)
-    width = early.shape[1] // 2
-    rows = late.shape[0]
-    lane = lax.broadcasted_iota(jnp.int32, (rows, width), 1)
-    late = jnp.concatenate([late, jnp.zeros((rows, width - 2 * line), jnp.float32)], axis=1)
-    halves = []
-    for index in range(2):
-        moved = turned(late, width - (1 + index) * line)
-        part = early[:, index * width : (index + 1) * width]
-        part = jnp.where(lane < width - line, part, moved)
-        step = count
-        while step < line:
-            part = part + turned(part, -step)
-            step *= 2
-        halves.append(part)
+    out_ref[...] = widened(products(left_ref, units, planes))
+
+
+def far_kernel(left_ref, near_ref, *refs, planes, flips, total_cells):
+    units, out_ref = refs[:-1], refs[-1]
+    count = units[0].shape[1]
+    near = near_ref[...] * (1.0 / total_cells)
+    far = widened(products(left_ref, units, planes)) * (1.0 / total_cells)
     dom, orb = lax.axis_index("dom"), lax.axis_index("orb")
     chip, core = orb >> 1, orb & 1
-    even = jnp.where(core == 0, halves[0], halves[1])
-    odd = jnp.where(core == 0, halves[1], halves[0])
-    joined = jnp.where(lane % line < count, even, turned(odd, count))
+    even = jnp.where(core == 0, near, far)
+    odd = jnp.where(core == 0, far, near)
+    lane = lax.broadcasted_iota(jnp.int32, even.shape, 1)
     for slot, flip in enumerate(flips):
-        out_ref[chip ^ flip ^ dom] = turned(joined, -slot * line)
+        block = jnp.where(
+            lane < count, turned(even, -slot * count), turned(odd, (1 - slot) * count)
+        )
+        out_ref[chip ^ flip ^ dom] = block
 
 
 def sum_kernel(*refs):
@@ -320,26 +302,23 @@
         name="filter",
     )(jnp.asarray(z_matrix()), *blocks)
 
-    first = flips[:-1]
     early = pl.pallas_call(
-        functools.partial(early_kernel, planes=planes, count=count),
-        out_shape=jax.ShapeDtypeStruct((2 * count, 2 * chips * planes * count), jnp.float32),
-        in_specs=[VMEM] * (1 + 2 * len(first)),
+        functools.partial(near_kernel, planes=planes),
+        out_shape=jax.ShapeDtypeStruct((2 * count, LANES), jnp.float32),
+        in_specs=[VMEM] * (1 + chips),
         out_specs=VMEM,
         compiler_params=SMALL,
         name="early",
-    )(left, *[near[flip] for flip in first], *[far[flip] for flip in first])
+    )(left, *[near[flip] for flip in flips])
 
     shares = pl.pallas_call(
-        functools.partial(
-            late_kernel, planes=planes, count=count, flips=flips, total_cells=total * cells
-        ),
+        functools.partial(far_kernel, planes=planes, flips=flips, total_cells=total * cells),
         out_shape=jax.ShapeDtypeStruct((doms, 2 * count, LANES), jnp.float32),
-        in_specs=[VMEM] * 4,
+        in_specs=[VMEM] * (2 + chips),
         out_specs=VMEM,
         compiler_params=SMALL,
         name="late",
-    )(left, early, near[flips[-1]], far[flips[-1]])
+    )(left, early, *[far[flip] for flip in flips])
     parts = [shares[0]] + [along_dom(shares[k], k) for k in range(1, doms)]
     return pl.pallas_call(
         sum_kernel,

time: 31.4 us -> 31.1 us (level)
  Pallas kernels: 6.39 us -> 6.04 us
    pallas_call x2, Pallas kernels: 1.02 us -> 0.66 us  [the longest x1 0.37 us: gathered_steps(): pl.pallas_call(functools.partial(far_kernel, planes=planes, flips=flips,...]
where the time goes in v1:
time: 31.1 us; the launch traced here: 30.9 us
  starting transfers between devices  15.2 us (49%)
  waiting for transfers between devices  9.58 us (31%)
  Pallas kernels  6.04 us (19%)
    ppermute x6, starting transfers between devices, along_dom(): return lax.ppermute(value, 'dom', [(i, i ^ step) for i in range(doms)])  8.09 us
    ppermute x7, starting transfers between devices, swap_orb(): return lax.ppermute(value, 'orb', [(i, i ^ flip) for i in range(orbs)])  7.14 us
    ppermute x7, waiting for transfers between devices, swap_orb(): return lax.ppermute(value, 'orb', [(i, i ^ flip) for i in range(orbs)])  5.54 us
    ppermute x6, waiting for transfers between devices, along_dom(): return lax.ppermute(value, 'dom', [(i, i ^ step) for i in range(doms)])  4.04 us
    pallas_call x1, Pallas kernels, gathered_steps(): pl.pallas_call(filter_kernel, out_shape=jax.ShapeDtypeStruct((planes * 2...  3.79 us
    pallas_call x1, Pallas kernels, gathered_steps(): pl.pallas_call(pack_kernel, out_shape=jax.ShapeDtypeStruct((planes + plan...  0.98 us
  transfers between devices with their start and end apart: 13, of which 4 were waited for; matrix products, arithmetic and copies ran while one was open for 0% of the time, Pallas kernels for 13%

profile of v1, /device:TPU:0, one launch (start us, length us, event | category | flops | bytes accessed | tf_op | source)
XLA Modules:
  0.0 30.9 jit_solution(4783112196889549279)
XLA Ops:
  0.0 1.0 %pack.1.refs_0_ = f32[10,4,768]{2,1,0:T(4,128)S(1)} custom-call(f32[8,4,768]{2,1,0:T(4,128)} %orbitals_ref.1, f32[8,768]{1,0:T(8,128)} %potential_ref.1), custom_call_target="tpu_custom_call" | custom-call | tf_op jit(solution)/shard_map/pack/pallas_call | solution.py:261
  1.0 3.0 %collective-permute-start = (f32[10,4,768]{2,1,0:T(4,128)S(1)}, f32[10,4,768]{2,1,0:T(4,128)S(1)}, u32[]{:S(2)}, u32[]{:S(2)}) collective-permute-start(f32[10,4,768]{2,1,0:T(4,128)S(1)} %pack.1.refs_0_), channel_id=1, source_target_pairs={{0,8},{8,0},{16,24},{24,16},{1,9},{9,1},{17,25},{25,17},{2,10},{10... | collective-permute-start | bytes 368648 | tf_op jit(solution)/shard_map/ppermute | solution.py:259
  4.0 1.5 %collective-permute-start.1 = (f32[10,4,768]{2,1,0:T(4,128)S(1)}, f32[10,4,768]{2,1,0:T(4,128)S(1)}, u32[]{:S(2)}, u32[]{:S(2)}) collective-permute-start(f32[10,4,768]{2,1,0:T(4,128)S(1)} %pack.1.refs_0_), channel_id=1, source_target_pairs={{0,16},{8,24},{16,0},{24,8},{1,17},{9,25},{17,1},{25,9},{2,18},{10... | collective-permute-start | bytes 368648 | tf_op jit(solution)/shard_map/ppermute | solution.py:259
  5.5 0.0 collective-permute-start.2
  5.6 3.0 %collective-permute-start.4 = (f32[8,4,768]{2,1,0:T(4,128)S(1)}, f32[8,4,768]{2,1,0:T(4,128)S(1)}, u32[]{:S(2)}, u32[]{:S(2)}) collective-permute-start(f32[8,4,768]{2,1,0:T(4,128)S(1)} %copy-done.1), channel_id=1, source_target_pairs={{0,4},{1,5},{2,6},{3,7},{4,0},{5,1},{6,2},{7,3},{8,12},{9,13},{10,... | collective-permute-start | bytes 294920 | tf_op jit(solution)/shard_map/ppermute | solution.py:256
  8.6 1.3 %collective-permute-start.5 = (f32[8,4,768]{2,1,0:T(4,128)S(1)}, f32[8,4,768]{2,1,0:T(4,128)S(1)}, u32[]{:S(2)}, u32[]{:S(2)}) collective-permute-start(f32[8,4,768]{2,1,0:T(4,128)S(1)} %copy-done.1), channel_id=1, source_target_pairs={{0,6},{1,7},{2,4},{3,5},{4,2},{5,3},{6,0},{7,1},{8,14},{9,15},{10,... | collective-permute-start | bytes 294920 | tf_op jit(solution)/shard_map/ppermute | solution.py:256
  10.0 5.5 %collective-permute-done.4.refs_2_ = f32[8,4,768]{2,1,0:T(4,128)S(1)} collective-permute-done((f32[8,4,768]{2,1,0:T(4,128)S(1)}, f32[8,4,768]{2,1,0:T(4,128)S(1)}, u32[]{:S(2)}, u32[]{:S(2)}) %collective-permute-start.4) | collective-permute-done | bytes 98336 | tf_op jit(solution)/shard_map/ppermute | solution.py:256
  15.5 0.1 collective-permute-start.3
  15.6 0.0 collective-permute-done.5.refs_3_
  15.6 0.0 collective-permute-start.6
  15.6 2.1 %collective-permute-start.7 = (f32[8,4,768]{2,1,0:T(4,128)S(1)}, f32[8,4,768]{2,1,0:T(4,128)S(1)}, u32[]{:S(2)}, u32[]{:S(2)}) collective-permute-start(f32[8,4,768]{2,1,0:T(4,128)S(1)} %copy-done.1), channel_id=1, source_target_pairs={{0,3},{1,2},{2,1},{3,0},{4,7},{5,6},{6,5},{7,4},{8,11},{9,10},{10,... | collective-permute-start | bytes 294920 | tf_op jit(solution)/shard_map/ppermute | solution.py:256
  17.7 0.0 collective-permute-start.8
  17.8 0.5 %collective-permute-start.9 = (f32[8,4,768]{2,1,0:T(4,128)S(1)}, f32[8,4,768]{2,1,0:T(4,128)S(1)}, u32[]{:S(2)}, u32[]{:S(2)}) collective-permute-start(f32[8,4,768]{2,1,0:T(4,128)S(1)} %collective-permute-done.5.refs_3_), channel_id=1, source_target_pairs={{0,1},{1,0},{2,3},{3,2},{4,5},{5,4},{6,7},{7,6},{8,9},{9,8},{10,11... | collective-permute-start | bytes 294920 | tf_op jit(solution)/shard_map/ppermute | solution.py:256
  18.3 3.8 %filter.1.left_ref = f32[64,768]{1,0:T(8,128)S(1)} custom-call(bf16[256,256]{1,0:T(8,128)(2,1)S(1)} %copy-done, f32[10,4,768]{2,1,0:T(4,128)S(1)} %pack.1.refs_0_, f32[10,4,768]{2,1,0:T(4,128)S(1)} %collective-permute-done.refs_1_, f32[10,4,768]{2,1,0:T(4,128)S(1)} %collective-permute-done.1.refs_2_, f32[10,4,768]{2,1,0:T(4,128)S(1)} %collective-permute-done.2.refs_3_), custom_call_target="tpu_custom_call" | custom-call | flops 25395200 | bytes 491520 | tf_op jit(solution)/shard_map/filter/pallas_call | solution.py:288
  22.1 0.3 early.1.near_ref
  22.4 0.0 collective-permute-done.8.refs_2_
  22.4 0.4 %late.1 = f32[4,8,128]{2,1,0:T(8,128)S(1)} custom-call(f32[64,768]{1,0:T(8,128)S(1)} %filter.1.left_ref, f32[8,128]{1,0:T(8,128)S(1)} %early.1.near_ref, f32[8,4,768]{2,1,0:T(4,128)S(1)} %collective-permute-done.6.refs_0_, f32[8,4,768]{2,1,0:T(4,128)S(1)} %collective-permute-done.7.refs_1_, f32[8,4,768]{2,1,0:T(4,128)S(1)} %collective-permute-done.8.refs_2_, ...), custom_call_target="tpu_custom_call" | custom-call | tf_op jit(solution)/shard_map/late/pallas_call | solution.py:314
  22.8 1.5 %collective-permute-start.10 = (f32[8,128]{1,0:T(8,128)S(1)}, f32[8,128]{1,0:T(8,128)S(1)}, u32[]{:S(2)}, u32[]{:S(2)}) collective-permute-start(f32[8,128]{1,0:T(8,128)S(1)} %get-tuple-element.7), channel_id=1, source_target_pairs={{0,8},{8,0},{16,24},{24,16},{1,9},{9,1},{17,25},{25,17},{2,10},{10... | collective-permute-start | bytes 12296 | tf_op jit(solution)/shard_map/ppermute | solution.py:259
  24.3 1.5 %collective-permute-start.11 = (f32[8,128]{1,0:T(8,128)S(1)}, f32[8,128]{1,0:T(8,128)S(1)}, u32[]{:S(2)}, u32[]{:S(2)}) collective-permute-start(f32[8,128]{1,0:T(8,128)S(1)} %get-tuple-element.6), channel_id=1, source_target_pairs={{0,16},{8,24},{16,0},{24,8},{1,17},{9,25},{17,1},{25,9},{2,18},{10... | collective-permute-start | bytes 12296 | tf_op jit(solution)/shard_map/ppermute | solution.py:259
  25.8 0.5 %collective-permute-start.12 = (f32[8,128]{1,0:T(8,128)S(1)}, f32[8,128]{1,0:T(8,128)S(1)}, u32[]{:S(2)}, u32[]{:S(2)}) collective-permute-start(f32[8,128]{1,0:T(8,128)S(1)} %get-tuple-element.5), channel_id=1, source_target_pairs={{0,24},{8,16},{16,8},{24,0},{1,25},{9,17},{17,9},{25,1},{2,26},{10... | collective-permute-start | bytes 12296 | tf_op jit(solution)/shard_map/ppermute | solution.py:259
  26.3 0.1 collective-permute-done.10.refs_1_
  26.4 1.5 %collective-permute-done.11.refs_2_ = f32[8,128]{1,0:T(8,128)S(1)} collective-permute-done((f32[8,128]{1,0:T(8,128)S(1)}, f32[8,128]{1,0:T(8,128)S(1)}, u32[]{:S(2)}, u32[]{:S(2)}) %collective-permute-start.11) | collective-permute-done | bytes 4128 | tf_op jit(solution)/shard_map/ppermute | solution.py:259
  27.9 2.4 %collective-permute-done.12.refs_3_ = f32[8,128]{1,0:T(8,128)S(1)} collective-permute-done((f32[8,128]{1,0:T(8,128)S(1)}, f32[8,128]{1,0:T(8,128)S(1)}, u32[]{:S(2)}, u32[]{:S(2)}) %collective-permute-start.12) | collective-permute-done | bytes 4128 | tf_op jit(solution)/shard_map/ppermute | solution.py:259
  30.3 0.6 %total.1 = f32[2,4,8]{2,1,0:T(4,128)} custom-call(f32[8,128]{1,0:T(8,128)S(1)} %get-tuple-element.8.refs_0_, f32[8,128]{1,0:T(8,128)S(1)} %collective-permute-done.10.refs_1_, f32[8,128]{1,0:T(8,128)S(1)} %collective-permute-done.11.refs_2_, f32[8,128]{1,0:T(8,128)S(1)} %collective-permute-done.12.refs_3_), custom_call_target="tpu_custom_call" | custom-call | tf_op jit(solution)/shard_map/total/pallas_call | solution.py:323
  (12 shorter events, 0.0 us)
Async XLA Ops:
  0.0 18.3 %copy-start = (bf16[256,256]{1,0:T(8,128)(2,1)S(1)}, bf16[256,256]{1,0:T(8,128)(2,1)}, u32[]{:S(2)}) copy-start(bf16[256,256]{1,0:T(8,128)(2,1)} %constant.2.clone.matrix_ref) | copy-start | bytes 393220
  0.0 5.6 %copy-start.1 = (f32[8,4,768]{2,1,0:T(4,128)S(1)}, f32[8,4,768]{2,1,0:T(4,128)}, u32[]{:S(2)}) copy-start(f32[8,4,768]{2,1,0:T(4,128)} %orbitals_ref.1) | copy-start | bytes 294916
  1.0 14.6 %collective-permute-start = (f32[10,4,768]{2,1,0:T(4,128)S(1)}, f32[10,4,768]{2,1,0:T(4,128)S(1)}, u32[]{:S(2)}, u32[]{:S(2)}) collective-permute-start(f32[10,4,768]{2,1,0:T(4,128)S(1)} %pack.1.refs_0_), channel_id=1, source_target_pairs={{0,8},{8,0},{16,24},{24,16},{1,9},{9,1},{17,25},{25,17},{2,10},{10... | collective-permute-start | bytes 368648 | tf_op jit(solution)/shard_map/ppermute | solution.py:259
  4.0 13.7 %collective-permute-start.1 = (f32[10,4,768]{2,1,0:T(4,128)S(1)}, f32[10,4,768]{2,1,0:T(4,128)S(1)}, u32[]{:S(2)}, u32[]{:S(2)}) collective-permute-start(f32[10,4,768]{2,1,0:T(4,128)S(1)} %pack.1.refs_0_), channel_id=1, source_target_pairs={{0,16},{8,24},{16,0},{24,8},{1,17},{9,25},{17,1},{25,9},{2,18},{10... | collective-permute-start | bytes 368648 | tf_op jit(solution)/shard_map/ppermute | solution.py:259
  5.5 12.2 %collective-permute-start.2 = (f32[10,4,768]{2,1,0:T(4,128)S(1)}, f32[10,4,768]{2,1,0:T(4,128)S(1)}, u32[]{:S(2)}, u32[]{:S(2)}) collective-permute-start(f32[10,4,768]{2,1,0:T(4,128)S(1)} %pack.1.refs_0_), channel_id=1, source_target_pairs={{0,24},{8,16},{16,8},{24,0},{1,25},{9,17},{17,9},{25,1},{2,26},{10... | collective-permute-start | bytes 368648 | tf_op jit(solution)/shard_map/ppermute | solution.py:259
  5.6 9.9 %collective-permute-start.4 = (f32[8,4,768]{2,1,0:T(4,128)S(1)}, f32[8,4,768]{2,1,0:T(4,128)S(1)}, u32[]{:S(2)}, u32[]{:S(2)}) collective-permute-start(f32[8,4,768]{2,1,0:T(4,128)S(1)} %copy-done.1), channel_id=1, source_target_pairs={{0,4},{1,5},{2,6},{3,7},{4,0},{5,1},{6,2},{7,3},{8,12},{9,13},{10,... | collective-permute-start | bytes 294920 | tf_op jit(solution)/shard_map/ppermute | solution.py:256
  8.6 7.0 %collective-permute-start.5 = (f32[8,4,768]{2,1,0:T(4,128)S(1)}, f32[8,4,768]{2,1,0:T(4,128)S(1)}, u32[]{:S(2)}, u32[]{:S(2)}) collective-permute-start(f32[8,4,768]{2,1,0:T(4,128)S(1)} %copy-done.1), channel_id=1, source_target_pairs={{0,6},{1,7},{2,4},{3,5},{4,2},{5,3},{6,0},{7,1},{8,14},{9,15},{10,... | collective-permute-start | bytes 294920 | tf_op jit(solution)/shard_map/ppermute | solution.py:256
  15.5 6.6 %collective-permute-start.3 = (f32[8,4,768]{2,1,0:T(4,128)S(1)}, f32[8,4,768]{2,1,0:T(4,128)S(1)}, u32[]{:S(2)}, u32[]{:S(2)}) collective-permute-start(f32[8,4,768]{2,1,0:T(4,128)S(1)} %copy-done.1), channel_id=1, source_target_pairs={{0,2},{1,3},{2,0},{3,1},{4,6},{5,7},{6,4},{7,5},{8,10},{9,11},{10,... | collective-permute-start | bytes 294920 | tf_op jit(solution)/shard_map/ppermute | solution.py:256
  15.6 6.8 %collective-permute-start.6 = (f32[8,4,768]{2,1,0:T(4,128)S(1)}, f32[8,4,768]{2,1,0:T(4,128)S(1)}, u32[]{:S(2)}, u32[]{:S(2)}) collective-permute-start(f32[8,4,768]{2,1,0:T(4,128)S(1)} %copy-done.1), channel_id=1, source_target_pairs={{0,1},{1,0},{2,3},{3,2},{4,5},{5,4},{6,7},{7,6},{8,9},{9,8},{10,11... | collective-permute-start | bytes 294920 | tf_op jit(solution)/shard_map/ppermute | solution.py:256
  15.6 6.8 %collective-permute-start.7 = (f32[8,4,768]{2,1,0:T(4,128)S(1)}, f32[8,4,768]{2,1,0:T(4,128)S(1)}, u32[]{:S(2)}, u32[]{:S(2)}) collective-permute-start(f32[8,4,768]{2,1,0:T(4,128)S(1)} %copy-done.1), channel_id=1, source_target_pairs={{0,3},{1,2},{2,1},{3,0},{4,7},{5,6},{6,5},{7,4},{8,11},{9,10},{10,... | collective-permute-start | bytes 294920 | tf_op jit(solution)/shard_map/ppermute | solution.py:256
  17.7 4.6 %collective-permute-start.8 = (f32[8,4,768]{2,1,0:T(4,128)S(1)}, f32[8,4,768]{2,1,0:T(4,128)S(1)}, u32[]{:S(2)}, u32[]{:S(2)}) collective-permute-start(f32[8,4,768]{2,1,0:T(4,128)S(1)} %collective-permute-done.4.refs_2_), channel_id=1, source_target_pairs={{0,1},{1,0},{2,3},{3,2},{4,5},{5,4},{6,7},{7,6},{8,9},{9,8},{10,11... | collective-permute-start | bytes 294920 | tf_op jit(solution)/shard_map/ppermute | solution.py:256
  17.8 4.6 %collective-permute-start.9 = (f32[8,4,768]{2,1,0:T(4,128)S(1)}, f32[8,4,768]{2,1,0:T(4,128)S(1)}, u32[]{:S(2)}, u32[]{:S(2)}) collective-permute-start(f32[8,4,768]{2,1,0:T(4,128)S(1)} %collective-permute-done.5.refs_3_), channel_id=1, source_target_pairs={{0,1},{1,0},{2,3},{3,2},{4,5},{5,4},{6,7},{7,6},{8,9},{9,8},{10,11... | collective-permute-start | bytes 294920 | tf_op jit(solution)/shard_map/ppermute | solution.py:256
  22.8 3.6 %collective-permute-start.10 = (f32[8,128]{1,0:T(8,128)S(1)}, f32[8,128]{1,0:T(8,128)S(1)}, u32[]{:S(2)}, u32[]{:S(2)}) collective-permute-start(f32[8,128]{1,0:T(8,128)S(1)} %get-tuple-element.7), channel_id=1, source_target_pairs={{0,8},{8,0},{16,24},{24,16},{1,9},{9,1},{17,25},{25,17},{2,10},{10... | collective-permute-start | bytes 12296 | tf_op jit(solution)/shard_map/ppermute | solution.py:259
  24.3 3.6 %collective-permute-start.11 = (f32[8,128]{1,0:T(8,128)S(1)}, f32[8,128]{1,0:T(8,128)S(1)}, u32[]{:S(2)}, u32[]{:S(2)}) collective-permute-start(f32[8,128]{1,0:T(8,128)S(1)} %get-tuple-element.6), channel_id=1, source_target_pairs={{0,16},{8,24},{16,0},{24,8},{1,17},{9,25},{17,1},{25,9},{2,18},{10... | collective-permute-start | bytes 12296 | tf_op jit(solution)/shard_map/ppermute | solution.py:259
  25.8 4.5 %collective-permute-start.12 = (f32[8,128]{1,0:T(8,128)S(1)}, f32[8,128]{1,0:T(8,128)S(1)}, u32[]{:S(2)}, u32[]{:S(2)}) collective-permute-start(f32[8,128]{1,0:T(8,128)S(1)} %get-tuple-element.5), channel_id=1, source_target_pairs={{0,24},{8,16},{16,8},{24,0},{1,25},{9,17},{17,9},{25,1},{2,26},{10... | collective-permute-start | bytes 12296 | tf_op jit(solution)/shard_map/ppermute | solution.py:259
